TPU v7x, 32 devices: a whole 2x2x4 slice. The times are simulated.
32 devices in a mesh: ma: 16 (over z, y, core), freq: 2 (over x).
Axes of the slice: x: 2, y: 2, z: 4, core: 2. Of those that a mesh axis runs over, the one named last changes fastest.
Arguments:
- right_side: float32 [128, 8, 2, 512], P('ma', 'freq'), may hold values from -60 to 60
- start_field: float32 [128, 8, 2, 512], P('ma', 'freq'), may hold values from -6 to 6
- beam: float32 [128, 8, 2, 16, 512], P('ma', 'freq'), may hold values from -0.75 to 0.75
- noise: float32 [128, 8, 16], P('ma', 'freq'), may hold values from 0.3 to 3
- inv_power: float32 [512], replicated, may hold values from 0.5 to 2
- smooth: float32 [512], replicated, may hold values from 0.5 to 4
Outputs:
- solution_field: float32 [128, 8, 2, 512], P('ma', 'freq')
- residual: float32 [128, 8, 2, 512], P('ma', 'freq')
All inputs are finite; a program needn't handle non-finite values.
Results may differ from a plain program's by a relative error of at most 0.0003.
Values sent between devices are 32-bit elements; how exact they have to be, the bound alone decides.
A program may use at most 64 MiB of HBM per device.

v0:
```python
import jax
import jax.numpy as jnp
from jax import lax
from jax.sharding import PartitionSpec as P

ITERS = 2


def extended(array, sides, width):
    for axis, dim in sides:
        size, length = (lax.axis_size(axis), array.shape[dim])
        up = [(i, (i + 1) % size) for i in range(size - 1)]
        down = [(j, i) for i, j in up]
        last = lax.slice_in_dim(array, length - width, length, axis=dim)
        leading = lax.slice_in_dim(array, 0, width, axis=dim)
        before = lax.ppermute(last, axis, up)
        after = lax.ppermute(leading, axis, down)
        array = jnp.concatenate([before, array, after], axis=dim)
    return array


def beam_image(field, beam, noise):
    projected = jnp.einsum("mfakl,mfbl->mfabk", beam, field, precision=lax.Precision.HIGHEST)
    real_part = projected[:, :, 0, 0] + projected[:, :, 1, 1]
    imaginary = projected[:, :, 0, 1] - projected[:, :, 1, 0]
    weighted = jnp.stack([real_part, imaginary], axis=2) * noise[:, :, None, :]
    back = jnp.einsum("mfakl,mfbk->mfabl", beam, weighted, precision=lax.Precision.HIGHEST)
    return jnp.stack(
        [back[:, :, 0, 0] - back[:, :, 1, 1], back[:, :, 0, 1] + back[:, :, 1, 0]], axis=2
    )


def prior_term(padded, field, first, total, smooth):
    channel = first + jnp.arange(field.shape[1], dtype=jnp.int32)
    weight = (channel > 0).astype(jnp.float32) + (channel < total - 1).astype(jnp.float32)
    return smooth * (weight[None, :, None, None] * field - padded[:, :-2] - padded[:, 2:])


def two_products(vector, applied):
    return lax.psum((jnp.sum(vector * vector), jnp.sum(vector * applied)), ("ma", "freq"))


def shards(right_side, start_field, beam, noise, inv_power, smooth):
    first = lax.axis_index("freq") * right_side.shape[1]
    total = right_side.shape[1] * lax.axis_size("freq")

    def padded_of(field):
        return extended(field, (("freq", 1),), 1)

    def operate(field):
        prior = prior_term(padded_of(field), field, first, total, smooth)
        return beam_image(field, beam, noise) + inv_power * field + prior

    solution = start_field
    resid_now = right_side - operate(start_field)
    applied = operate(resid_now)
    norm_now, curve_now = two_products(resid_now, applied)
    step_size = norm_now / curve_now
    direction = resid_now
    along = applied
    for turn in range(ITERS):
        solution = solution + step_size * direction
        resid_now = resid_now - step_size * along
        if turn + 1 < ITERS:
            applied = operate(resid_now)
            norm_next, curve_now = two_products(resid_now, applied)
            growth = norm_next / norm_now
            step_size = norm_next / (curve_now - growth * norm_next / step_size)
            direction = resid_now + growth * direction
            along = applied + growth * along
            norm_now = norm_next
    return (solution, resid_now)


def solution(mesh):
    in_specs = (
        P("ma", "freq", None, None),
        P("ma", "freq", None, None),
        P("ma", "freq", None, None, None),
        P("ma", "freq", None),
        P(),
        P(),
    )
    out_specs = (P("ma", "freq", None, None), P("ma", "freq", None, None))
    return jax.shard_map(shards, mesh=mesh, in_specs=in_specs, out_specs=out_specs, check_vma=False)
```

profile of v0, /device:TPU:0, one launch (start us, length us, event | category | flops | bytes accessed | tf_op | source)
XLA Modules:
  0.0 144.0 jit_solution(10948142598104500641)
XLA Ops:
  0.6 0.0 copy-start
  0.7 0.9 fusion.42
  1.6 4.9 %collective-permute-start = (f32[8,1,2,512]{3,2,1,0:T(2,128)S(1)}, f32[8,1,2,512]{3,2,1,0:T(2,128)S(1)}, u32[]{:S(2)}, u32[]{:S(2)}) collective-permute-start(f32[8,1,2,512]{3,2,1,0:T(2,128)S(1)} %get-tuple-element.22), channel_id=1, source_target_pairs={{0,1},{2,3},{4,5},{6,7},{8,9},{10,11},{12,13},{14,15},{16,17},{18,... | collective-permute-start | bytes 98312 | tf_op jit(solution)/shard_map/ppermute | solution.py:16
  6.5 1.3 collective-permute-start.1
  7.8 8.3 %convolution_bitcast_fusion.1 = f32[8,4,2,2,16]{4,3,2,1,0:T(2,128)S(1)} fusion(f32[8,4,2,16,512]{4,3,2,1,0:T(8,128)S(1)} %copy-done, f32[8,4,2,512]{3,2,1,0:T(2,128)} %param.7), kind=kOutput, calls=%fused_computation.1 | convolution fusion | flops 12582912 | bytes 2236416 | tf_op jit(solution)/shard_map/mfakl,mfbl->mfabk/dot_general | solution.py:23
  16.1 0.0 copy-start.4
  16.1 0.0 copy-start.5
  16.2 1.1 convolution_bitcast_fusion
  17.3 0.1 fusion.22
  17.4 0.1 fusion.24
  17.6 0.3 fusion.11
  17.9 7.4 %fusion.15 = f32[8,4,2,2,16]{4,2,3,1,0:T(2,128)S(1)} fusion(f32[8,4,2,16,512]{4,3,2,1,0:T(8,128)S(1)} %copy-done, f32[8,4,2,512]{3,2,1,0:T(2,128)S(1)} %fusion.11), kind=kOutput, calls=%fused_computation.28 | convolution fusion | flops 12582912 | bytes 2236416 | tf_op jit(solution)/shard_map/mfakl,mfbl->mfabk/dot_general | solution.py:23
  25.4 1.3 fusion.30
  26.7 0.1 copy.46
  26.9 4.5 %collective-permute-start.2 = (f32[8,1,2,512]{3,2,1,0:T(2,128)S(1)}, f32[8,1,2,512]{3,2,1,0:T(2,128)S(1)}, u32[]{:S(2)}, u32[]{:S(2)}) collective-permute-start(f32[8,1,2,512]{3,2,1,0:T(2,128)S(1)} %get-tuple-element.20), channel_id=1, source_target_pairs={{0,1},{2,3},{4,5},{6,7},{8,9},{10,11},{12,13},{14,15},{16,17},{18,... | collective-permute-start | bytes 98312 | tf_op jit(solution)/shard_map/ppermute | solution.py:16
  31.4 1.3 collective-permute-start.3
  32.7 0.1 fusion.21
  32.9 0.1 collective-permute-done.2
  33.0 4.2 %collective-permute-done.3 = f32[8,1,2,512]{3,2,1,0:T(2,128)S(1)} collective-permute-done((f32[8,1,2,512]{3,2,1,0:T(2,128)S(1)}, f32[8,1,2,512]{3,2,1,0:T(2,128)S(1)}, u32[]{:S(2)}, u32[]{:S(2)}) %collective-permute-start.3) | collective-permute-done | bytes 32800 | tf_op jit(solution)/shard_map/ppermute | solution.py:17
  37.2 1.1 multiply_reduce_fusion.2
  38.3 39.8 %all-reduce.1 = (f32[]{:T(128)}, f32[]{:T(128)}) all-reduce(f32[]{:T(128)} %get-tuple-element.5, f32[]{:T(128)} %get-tuple-element.4), channel_id=1, replica_groups=mesh['ma'=16,'freq'=2] {'ma','freq'}, use_global_device_ids=true, to_apply=%region_1.0 | all-reduce | flops 2 | bytes 16 | tf_op jit(solution)/shard_map/psum | solution.py:40
  79.4 7.4 %fusion.13 = f32[8,4,2,2,16]{4,2,3,1,0:T(2,128)S(1)} fusion(f32[8,4,2,16,512]{4,3,2,1,0:T(8,128)S(1)} %copy-done, f32[8,4,2,512]{3,2,1,0:T(2,128)S(1)} %bitcast.90), kind=kOutput, calls=%fused_computation.26 | convolution fusion | flops 12582912 | bytes 2236416 | tf_op jit(solution)/shard_map/mfakl,mfbl->mfabk/dot_general | solution.py:23
  86.9 1.1 fusion.28
  88.0 0.1 copy.45
  88.2 4.2 %collective-permute-start.4 = (f32[8,1,2,512]{3,2,1,0:T(2,128)S(1)}, f32[8,1,2,512]{3,2,1,0:T(2,128)S(1)}, u32[]{:S(2)}, u32[]{:S(2)}) collective-permute-start(f32[8,1,2,512]{3,2,1,0:T(2,128)S(1)} %get-tuple-element.18), channel_id=1, source_target_pairs={{0,1},{2,3},{4,5},{6,7},{8,9},{10,11},{12,13},{14,15},{16,17},{18,... | collective-permute-start | bytes 98312 | tf_op jit(solution)/shard_map/ppermute | solution.py:16
  92.4 1.3 collective-permute-start.5
  93.7 0.1 fusion.19
  93.8 0.1 collective-permute-done.4
  93.9 4.2 %collective-permute-done.5 = f32[8,1,2,512]{3,2,1,0:T(2,128)S(1)} collective-permute-done((f32[8,1,2,512]{3,2,1,0:T(2,128)S(1)}, f32[8,1,2,512]{3,2,1,0:T(2,128)S(1)}, u32[]{:S(2)}, u32[]{:S(2)}) %collective-permute-start.5) | collective-permute-done | bytes 32800 | tf_op jit(solution)/shard_map/ppermute | solution.py:17
  98.2 1.1 multiply_reduce_fusion
  99.3 39.4 %all-reduce = (f32[]{:T(128)}, f32[]{:T(128)}) all-reduce(f32[]{:T(128)} %get-tuple-element.3, f32[]{:T(128)} %get-tuple-element.2), channel_id=1, replica_groups=mesh['ma'=16,'freq'=2] {'ma','freq'}, use_global_device_ids=true, to_apply=%region_5.0 | all-reduce | flops 2 | bytes 16 | tf_op jit(solution)/shard_map/psum | solution.py:40
  143.3 0.8 multiply_subtract_fusion
  (24 shorter events, 0.2 us)
Async XLA Ops:
  0.6 7.1 %copy-start = (f32[8,4,2,16,512]{4,3,2,1,0:T(8,128)S(1)}, f32[8,4,2,16,512]{4,3,2,1,0:T(8,128)}, u32[]{:S(2)}) copy-start(f32[8,4,2,16,512]{4,3,2,1,0:T(8,128)} %param.8) | copy-start | bytes 6291460
  0.6 15.5 %copy-start.2 = (f32[8,4,16]{2,1,0:T(4,128)S(1)}, f32[8,4,16]{2,1,0:T(4,128)}, u32[]{:S(2)}) copy-start(f32[8,4,16]{2,1,0:T(4,128)} %param.9) | copy-start | bytes 6148
  1.6 16.0 %collective-permute-start = (f32[8,1,2,512]{3,2,1,0:T(2,128)S(1)}, f32[8,1,2,512]{3,2,1,0:T(2,128)S(1)}, u32[]{:S(2)}, u32[]{:S(2)}) collective-permute-start(f32[8,1,2,512]{3,2,1,0:T(2,128)S(1)} %get-tuple-element.22), channel_id=1, source_target_pairs={{0,1},{2,3},{4,5},{6,7},{8,9},{10,11},{12,13},{14,15},{16,17},{18,... | collective-permute-start | bytes 98312 | tf_op jit(solution)/shard_map/ppermute | solution.py:16
  6.5 11.1 %collective-permute-start.1 = (f32[8,1,2,512]{3,2,1,0:T(2,128)S(1)}, f32[8,1,2,512]{3,2,1,0:T(2,128)S(1)}, u32[]{:S(2)}, u32[]{:S(2)}) collective-permute-start(f32[8,1,2,512]{3,2,1,0:T(2,128)S(1)} %get-tuple-element.23), channel_id=1, source_target_pairs={{1,0},{3,2},{5,4},{7,6},{9,8},{11,10},{13,12},{15,14},{17,16},{19,... | collective-permute-start | bytes 98312 | tf_op jit(solution)/shard_map/ppermute | solution.py:17
  16.1 1.5 %copy-start.1 = (f32[8,4,2,512]{3,2,1,0:T(2,128)S(1)}, f32[8,4,2,512]{3,2,1,0:T(2,128)}, u32[]{:S(2)}) copy-start(f32[8,4,2,512]{3,2,1,0:T(2,128)} %param.7) | copy-start | bytes 393220
  16.1 1.5 %copy-start.3 = (f32[8,4,2,512]{3,2,1,0:T(2,128)S(1)}, f32[8,4,2,512]{3,2,1,0:T(2,128)}, u32[]{:S(2)}) copy-start(f32[8,4,2,512]{3,2,1,0:T(2,128)} %param.6) | copy-start | bytes 393220
  16.1 1.6 %copy-start.4 = (f32[512]{0:T(512)S(1)}, f32[512]{0:T(512)}, u32[]{:S(2)}) copy-start(f32[512]{0:T(512)} %param.11) | copy-start | bytes 6148
  16.1 1.5 %copy-start.5 = (f32[512]{0:T(512)S(1)}, f32[512]{0:T(512)}, u32[]{:S(2)}) copy-start(f32[512]{0:T(512)} %param.10) | copy-start | bytes 6148
  26.9 6.1 %collective-permute-start.2 = (f32[8,1,2,512]{3,2,1,0:T(2,128)S(1)}, f32[8,1,2,512]{3,2,1,0:T(2,128)S(1)}, u32[]{:S(2)}, u32[]{:S(2)}) collective-permute-start(f32[8,1,2,512]{3,2,1,0:T(2,128)S(1)} %get-tuple-element.20), channel_id=1, source_target_pairs={{0,1},{2,3},{4,5},{6,7},{8,9},{10,11},{12,13},{14,15},{16,17},{18,... | collective-permute-start | bytes 98312 | tf_op jit(solution)/shard_map/ppermute | solution.py:16
  31.4 5.8 %collective-permute-start.3 = (f32[8,1,2,512]{3,2,1,0:T(2,128)S(1)}, f32[8,1,2,512]{3,2,1,0:T(2,128)S(1)}, u32[]{:S(2)}, u32[]{:S(2)}) collective-permute-start(f32[8,1,2,512]{3,2,1,0:T(2,128)S(1)} %get-tuple-element.21), channel_id=1, source_target_pairs={{1,0},{3,2},{5,4},{7,6},{9,8},{11,10},{13,12},{15,14},{17,16},{19,... | collective-permute-start | bytes 98312 | tf_op jit(solution)/shard_map/ppermute | solution.py:17
  88.2 5.8 %collective-permute-start.4 = (f32[8,1,2,512]{3,2,1,0:T(2,128)S(1)}, f32[8,1,2,512]{3,2,1,0:T(2,128)S(1)}, u32[]{:S(2)}, u32[]{:S(2)}) collective-permute-start(f32[8,1,2,512]{3,2,1,0:T(2,128)S(1)} %get-tuple-element.18), channel_id=1, source_target_pairs={{0,1},{2,3},{4,5},{6,7},{8,9},{10,11},{12,13},{14,15},{16,17},{18,... | collective-permute-start | bytes 98312 | tf_op jit(solution)/shard_map/ppermute | solution.py:16
  92.4 5.8 %collective-permute-start.5 = (f32[8,1,2,512]{3,2,1,0:T(2,128)S(1)}, f32[8,1,2,512]{3,2,1,0:T(2,128)S(1)}, u32[]{:S(2)}, u32[]{:S(2)}) collective-permute-start(f32[8,1,2,512]{3,2,1,0:T(2,128)S(1)} %get-tuple-element.19), channel_id=1, source_target_pairs={{1,0},{3,2},{5,4},{7,6},{9,8},{11,10},{13,12},{15,14},{17,16},{19,... | collective-permute-start | bytes 98312 | tf_op jit(solution)/shard_map/ppermute | solution.py:17
where the time goes:
time: 145 us; the launch traced here: 144 us
  blocking collectives  79.2 us (55%)
  matrix products  26.7 us (18%)
  starting transfers between devices  17.5 us (12%)
  waiting for transfers between devices  8.73 us (6%)
  between operations  6.85 us (5%)
  other arithmetic  3.86 us (3%)
    psum x2, blocking collectives, two_products(): lax.psum((jnp.sum(vector * vector), jnp.sum(vector * applied)), ('ma', 'f...  79.2 us
    dot_general x3, matrix products, beam_image(): jnp.einsum('mfakl,mfbl->mfabk', beam, field, precision=lax.Precision.HIGH...  23.1 us
    ppermute x3, starting transfers between devices, extended(): before = lax.ppermute(last, axis, up)  13.6 us
    ppermute x3, waiting for transfers between devices, extended(): after = lax.ppermute(leading, axis, down)  8.46 us
    ppermute x3, starting transfers between devices, extended(): after = lax.ppermute(leading, axis, down)  3.88 us
    dot_general x3, matrix products, beam_image(): jnp.einsum('mfakl,mfbk->mfabl', beam, weighted, precision=lax.Precision.H...  3.6 us
  transfers between devices with their start and end apart: 6, of which 4 were waited for; matrix products, arithmetic and copies ran while one was open for 7% of the time, Pallas kernels for 0%

commit v1 on v0

--- a/solution.py
+++ b/solution.py
@@ -1,9 +1,19 @@
+import functools
 import jax
 import jax.numpy as jnp
 from jax import lax
 from jax.sharding import PartitionSpec as P
 
 ITERS = 2
+
+
+def assign_records_all(inp, link_axis, dev_axis):
+    for dev in (link_axis, dev_axis):
+        inp = jax.lax.psum(inp, dev)
+    return inp
+
+
+arrange_shapes_all = functools.partial(assign_records_all, link_axis="ma", dev_axis="freq")
 
 
 def extended(array, sides, width):
@@ -37,7 +47,7 @@
 
 
 def two_products(vector, applied):
-    return lax.psum((jnp.sum(vector * vector), jnp.sum(vector * applied)), ("ma", "freq"))
+    return arrange_shapes_all((jnp.sum(vector * vector), jnp.sum(vector * applied)))
 
 
 def shards(right_side, start_field, beam, noise, inv_power, smooth):

time: 145 us -> 136 us (0.938)
  blocking collectives: 79.2 us -> 73.4 us
  starting transfers between devices: 17.5 us -> 15.2 us
    psum x2 -> x4, blocking collectives: 79.2 us -> 73.4 us  [assign_records_all(): inp = jax.lax.psum(inp, dev)]
    ppermute x3, starting transfers between devices: 13.6 us -> 11.3 us  [extended(): before = lax.ppermute(last, axis, up)]
where the time goes in v1:
time: 136 us
  blocking collectives  73.4 us (54%)
  matrix products  26.7 us (20%)
  starting transfers between devices  15.2 us (11%)
  waiting for transfers between devices  8.73 us (6%)
  between operations  6.7 us (5%)
  other arithmetic  3.87 us (3%)
    psum x4, blocking collectives, assign_records_all(): inp = jax.lax.psum(inp, dev)  73.4 us
    dot_general x3, matrix products, beam_image(): jnp.einsum('mfakl,mfbl->mfabk', beam, field, precision=lax.Precision.HIGH...  23.1 us
    ppermute x3, starting transfers between devices, extended(): before = lax.ppermute(last, axis, up)  11.3 us
    ppermute x3, waiting for transfers between devices, extended(): after = lax.ppermute(leading, axis, down)  8.46 us
    ppermute x3, starting transfers between devices, extended(): after = lax.ppermute(leading, axis, down)  3.88 us
    dot_general x3, matrix products, beam_image(): jnp.einsum('mfakl,mfbk->mfabl', beam, weighted, precision=lax.Precision.H...  3.6 us
  transfers between devices with their start and end apart: 6, of which 4 were waited for; matrix products, arithmetic and copies ran while one was open for 7% of the time, Pallas kernels for 0%

profile of v1, /device:TPU:0, one launch (start us, length us, event | category | flops | bytes accessed | tf_op | source)
XLA Modules:
  0.0 135.9 jit_solution(16923702182581727259)
XLA Ops:
  0.7 0.9 fusion.42
  1.6 4.9 %collective-permute-start = (f32[8,1,2,512]{3,2,1,0:T(2,128)S(1)}, f32[8,1,2,512]{3,2,1,0:T(2,128)S(1)}, u32[]{:S(2)}, u32[]{:S(2)}) collective-permute-start(f32[8,1,2,512]{3,2,1,0:T(2,128)S(1)} %get-tuple-element.26), channel_id=1, source_target_pairs={{0,1},{2,3},{4,5},{6,7},{8,9},{10,11},{12,13},{14,15},{16,17},{18,... | collective-permute-start | bytes 98312 | tf_op jit(solution)/shard_map/ppermute | solution.py:26
  6.5 1.3 collective-permute-start.1
  7.8 8.3 %convolution_bitcast_fusion.1 = f32[8,4,2,2,16]{4,3,2,1,0:T(2,128)S(1)} fusion(f32[8,4,2,16,512]{4,3,2,1,0:T(8,128)S(1)} %copy-done, f32[8,4,2,512]{3,2,1,0:T(2,128)} %param.7), kind=kOutput, calls=%fused_computation.1 | convolution fusion | flops 12582912 | bytes 2236416 | tf_op jit(solution)/shard_map/mfakl,mfbl->mfabk/dot_general | solution.py:33
  16.1 0.0 copy-start.4
  16.2 1.1 convolution_bitcast_fusion
  17.3 0.1 fusion.22
  17.4 0.1 fusion.24
  17.6 0.3 fusion.11
  17.9 7.4 %fusion.15 = f32[8,4,2,2,16]{4,2,3,1,0:T(2,128)S(1)} fusion(f32[8,4,2,16,512]{4,3,2,1,0:T(8,128)S(1)} %copy-done, f32[8,4,2,512]{3,2,1,0:T(2,128)S(1)} %fusion.11), kind=kOutput, calls=%fused_computation.28 | convolution fusion | flops 12582912 | bytes 2236416 | tf_op jit(solution)/shard_map/mfakl,mfbl->mfabk/dot_general | solution.py:33
  25.4 1.3 fusion.30
  26.7 0.1 copy.46
  26.9 4.5 %collective-permute-start.2 = (f32[8,1,2,512]{3,2,1,0:T(2,128)S(1)}, f32[8,1,2,512]{3,2,1,0:T(2,128)S(1)}, u32[]{:S(2)}, u32[]{:S(2)}) collective-permute-start(f32[8,1,2,512]{3,2,1,0:T(2,128)S(1)} %get-tuple-element.24), channel_id=1, source_target_pairs={{0,1},{2,3},{4,5},{6,7},{8,9},{10,11},{12,13},{14,15},{16,17},{18,... | collective-permute-start | bytes 98312 | tf_op jit(solution)/shard_map/ppermute | solution.py:26
  31.4 1.3 collective-permute-start.3
  32.7 0.1 fusion.21
  32.9 0.1 collective-permute-done.2
  33.0 4.2 %collective-permute-done.3 = f32[8,1,2,512]{3,2,1,0:T(2,128)S(1)} collective-permute-done((f32[8,1,2,512]{3,2,1,0:T(2,128)S(1)}, f32[8,1,2,512]{3,2,1,0:T(2,128)S(1)}, u32[]{:S(2)}, u32[]{:S(2)}) %collective-permute-start.3) | collective-permute-done | bytes 32800 | tf_op jit(solution)/shard_map/ppermute | solution.py:27
  37.2 1.1 multiply_reduce_fusion.2
  38.3 32.1 %all-reduce.1 = (f32[]{:T(128)}, f32[]{:T(128)}) all-reduce(f32[]{:T(128)} %get-tuple-element.5, f32[]{:T(128)} %get-tuple-element.4), channel_id=1, replica_groups=mesh['ma'=16,'freq'=2] {'ma'}, use_global_device_ids=true, to_apply=%region_1.0 | all-reduce | flops 2 | bytes 16 | tf_op jit(solution)/shard_map/psum | solution.py:12
  70.4 5.5 %all-reduce.3 = (f32[]{:T(128)}, f32[]{:T(128)}) all-reduce(f32[]{:T(128)} %get-tuple-element.8, f32[]{:T(128)} %get-tuple-element.9), channel_id=1, replica_groups=mesh['ma'=16,'freq'=2] {'freq'}, use_global_device_ids=true, to_apply=%region_2.0 | all-reduce | flops 2 | bytes 16 | tf_op jit(solution)/shard_map/psum | solution.py:12
  77.3 7.4 %fusion.13 = f32[8,4,2,2,16]{4,2,3,1,0:T(2,128)S(1)} fusion(f32[8,4,2,16,512]{4,3,2,1,0:T(8,128)S(1)} %copy-done, f32[8,4,2,512]{3,2,1,0:T(2,128)S(1)} %bitcast.90), kind=kOutput, calls=%fused_computation.26 | convolution fusion | flops 12582912 | bytes 2236416 | tf_op jit(solution)/shard_map/mfakl,mfbl->mfabk/dot_general | solution.py:33
  84.8 1.1 fusion.28
  85.9 0.1 copy.45
  86.1 1.9 %collective-permute-start.4 = (f32[8,1,2,512]{3,2,1,0:T(2,128)S(1)}, f32[8,1,2,512]{3,2,1,0:T(2,128)S(1)}, u32[]{:S(2)}, u32[]{:S(2)}) collective-permute-start(f32[8,1,2,512]{3,2,1,0:T(2,128)S(1)} %get-tuple-element.22), channel_id=1, source_target_pairs={{0,1},{2,3},{4,5},{6,7},{8,9},{10,11},{12,13},{14,15},{16,17},{18,... | collective-permute-start | bytes 98312 | tf_op jit(solution)/shard_map/ppermute | solution.py:26
  88.0 1.3 collective-permute-start.5
  89.3 0.1 fusion.19
  89.4 0.1 collective-permute-done.4
  89.6 4.2 %collective-permute-done.5 = f32[8,1,2,512]{3,2,1,0:T(2,128)S(1)} collective-permute-done((f32[8,1,2,512]{3,2,1,0:T(2,128)S(1)}, f32[8,1,2,512]{3,2,1,0:T(2,128)S(1)}, u32[]{:S(2)}, u32[]{:S(2)}) %collective-permute-start.5) | collective-permute-done | bytes 32800 | tf_op jit(solution)/shard_map/ppermute | solution.py:27
  93.8 1.1 multiply_reduce_fusion
  95.0 30.1 %all-reduce = (f32[]{:T(128)}, f32[]{:T(128)}) all-reduce(f32[]{:T(128)} %get-tuple-element.3, f32[]{:T(128)} %get-tuple-element.2), channel_id=1, replica_groups=mesh['ma'=16,'freq'=2] {'ma'}, use_global_device_ids=true, to_apply=%region_7.0 | all-reduce | flops 2 | bytes 16 | tf_op jit(solution)/shard_map/psum | solution.py:12
  125.1 5.6 %all-reduce.2 = (f32[]{:T(128)}, f32[]{:T(128)}) all-reduce(f32[]{:T(128)} %get-tuple-element.6, f32[]{:T(128)} %get-tuple-element.7), channel_id=1, replica_groups=mesh['ma'=16,'freq'=2] {'freq'}, use_global_device_ids=true, to_apply=%region_8.0 | all-reduce | flops 2 | bytes 16 | tf_op jit(solution)/shard_map/psum | solution.py:12
  135.1 0.8 multiply_subtract_fusion
  (26 shorter events, 0.2 us)
Async XLA Ops:
  0.6 7.1 %copy-start = (f32[8,4,2,16,512]{4,3,2,1,0:T(8,128)S(1)}, f32[8,4,2,16,512]{4,3,2,1,0:T(8,128)}, u32[]{:S(2)}) copy-start(f32[8,4,2,16,512]{4,3,2,1,0:T(8,128)} %param.8) | copy-start | bytes 6291460
  0.6 15.5 %copy-start.2 = (f32[8,4,16]{2,1,0:T(4,128)S(1)}, f32[8,4,16]{2,1,0:T(4,128)}, u32[]{:S(2)}) copy-start(f32[8,4,16]{2,1,0:T(4,128)} %param.9) | copy-start | bytes 6148
  1.6 16.0 %collective-permute-start = (f32[8,1,2,512]{3,2,1,0:T(2,128)S(1)}, f32[8,1,2,512]{3,2,1,0:T(2,128)S(1)}, u32[]{:S(2)}, u32[]{:S(2)}) collective-permute-start(f32[8,1,2,512]{3,2,1,0:T(2,128)S(1)} %get-tuple-element.26), channel_id=1, source_target_pairs={{0,1},{2,3},{4,5},{6,7},{8,9},{10,11},{12,13},{14,15},{16,17},{18,... | collective-permute-start | bytes 98312 | tf_op jit(solution)/shard_map/ppermute | solution.py:26
  6.5 11.1 %collective-permute-start.1 = (f32[8,1,2,512]{3,2,1,0:T(2,128)S(1)}, f32[8,1,2,512]{3,2,1,0:T(2,128)S(1)}, u32[]{:S(2)}, u32[]{:S(2)}) collective-permute-start(f32[8,1,2,512]{3,2,1,0:T(2,128)S(1)} %get-tuple-element.27), channel_id=1, source_target_pairs={{1,0},{3,2},{5,4},{7,6},{9,8},{11,10},{13,12},{15,14},{17,16},{19,... | collective-permute-start | bytes 98312 | tf_op jit(solution)/shard_map/ppermute | solution.py:27
  16.1 1.5 %copy-start.1 = (f32[8,4,2,512]{3,2,1,0:T(2,128)S(1)}, f32[8,4,2,512]{3,2,1,0:T(2,128)}, u32[]{:S(2)}) copy-start(f32[8,4,2,512]{3,2,1,0:T(2,128)} %param.7) | copy-start | bytes 393220
  16.1 1.5 %copy-start.3 = (f32[8,4,2,512]{3,2,1,0:T(2,128)S(1)}, f32[8,4,2,512]{3,2,1,0:T(2,128)}, u32[]{:S(2)}) copy-start(f32[8,4,2,512]{3,2,1,0:T(2,128)} %param.6) | copy-start | bytes 393220
  16.1 1.6 %copy-start.4 = (f32[512]{0:T(512)S(1)}, f32[512]{0:T(512)}, u32[]{:S(2)}) copy-start(f32[512]{0:T(512)} %param.11) | copy-start | bytes 6148
  16.1 1.5 %copy-start.5 = (f32[512]{0:T(512)S(1)}, f32[512]{0:T(512)}, u32[]{:S(2)}) copy-start(f32[512]{0:T(512)} %param.10) | copy-start | bytes 6148
  26.9 6.1 %collective-permute-start.2 = (f32[8,1,2,512]{3,2,1,0:T(2,128)S(1)}, f32[8,1,2,512]{3,2,1,0:T(2,128)S(1)}, u32[]{:S(2)}, u32[]{:S(2)}) collective-permute-start(f32[8,1,2,512]{3,2,1,0:T(2,128)S(1)} %get-tuple-element.24), channel_id=1, source_target_pairs={{0,1},{2,3},{4,5},{6,7},{8,9},{10,11},{12,13},{14,15},{16,17},{18,... | collective-permute-start | bytes 98312 | tf_op jit(solution)/shard_map/ppermute | solution.py:26
  31.4 5.8 %collective-permute-start.3 = (f32[8,1,2,512]{3,2,1,0:T(2,128)S(1)}, f32[8,1,2,512]{3,2,1,0:T(2,128)S(1)}, u32[]{:S(2)}, u32[]{:S(2)}) collective-permute-start(f32[8,1,2,512]{3,2,1,0:T(2,128)S(1)} %get-tuple-element.25), channel_id=1, source_target_pairs={{1,0},{3,2},{5,4},{7,6},{9,8},{11,10},{13,12},{15,14},{17,16},{19,... | collective-permute-start | bytes 98312 | tf_op jit(solution)/shard_map/ppermute | solution.py:27
  86.1 3.5 %collective-permute-start.4 = (f32[8,1,2,512]{3,2,1,0:T(2,128)S(1)}, f32[8,1,2,512]{3,2,1,0:T(2,128)S(1)}, u32[]{:S(2)}, u32[]{:S(2)}) collective-permute-start(f32[8,1,2,512]{3,2,1,0:T(2,128)S(1)} %get-tuple-element.22), channel_id=1, source_target_pairs={{0,1},{2,3},{4,5},{6,7},{8,9},{10,11},{12,13},{14,15},{16,17},{18,... | collective-permute-start | bytes 98312 | tf_op jit(solution)/shard_map/ppermute | solution.py:26
  88.0 5.8 %collective-permute-start.5 = (f32[8,1,2,512]{3,2,1,0:T(2,128)S(1)}, f32[8,1,2,512]{3,2,1,0:T(2,128)S(1)}, u32[]{:S(2)}, u32[]{:S(2)}) collective-permute-start(f32[8,1,2,512]{3,2,1,0:T(2,128)S(1)} %get-tuple-element.23), channel_id=1, source_target_pairs={{1,0},{3,2},{5,4},{7,6},{9,8},{11,10},{13,12},{15,14},{17,16},{19,... | collective-permute-start | bytes 98312 | tf_op jit(solution)/shard_map/ppermute | solution.py:27
